TPU v7x, 256 devices: a whole 4x4x8 slice. The times are simulated.
256 devices in a mesh: section: 4 (over x), expert: 64 (over z, y, core).
Axes of the slice: x: 4, y: 4, z: 8, core: 2. Of those that a mesh axis runs over, the one named last changes fastest.
Arguments:
- embedded: bfloat16 [4, 1024, 7168], P('section', 'expert'), may hold values from -6 to 6
- norm_gain: float32 [4, 7168], P('section'), may hold values from 0.1 to 1.9
- gate_proj: bfloat16 [4, 7168, 16384], P('section', None, 'expert'), may hold values from -0.0625 to 0.0625
- up_proj: bfloat16 [4, 7168, 16384], P('section', None, 'expert'), may hold values from -0.0625 to 0.0625
- down_proj: bfloat16 [4, 16384, 7168], P('section', 'expert'), may hold values from -0.125 to 0.125
- expert_ids: int32 [4, 4, 1024, 8], P('section', None, 'expert'), may hold values from 0 to 255, all different within a row; in each aligned block of 16 rows (0 to 15, 16 to 31, ..., all dimensions but the last counted through in order) at most 2 rows name the same one
- route_gates: float32 [4, 4, 1024, 8], P('section', None, 'expert'), may hold values from 0.2 to 2.5
Outputs:
- processed: bfloat16 [4, 1024, 7168], P('section', 'expert')
Inputs may be any that keep to these rules, and one draw needn't show every extreme that they name: `expert_ids`: each row names 8 different experts; within one layer and micro-batch no expert is named by more than 2 tokens of an aligned block of 16 tokens.
All inputs are finite; a program needn't handle non-finite values.
Results may differ from a plain program's by a relative error of at most 0.0085.
Values may be sent and summed in bfloat16 or wider, within the bound.
A program may use at most 128 MiB of HBM per device.

v0:
```python
import jax
import jax.numpy as jnp
from jax import lax
from jax.sharding import PartitionSpec as P

CAP = 2


eps_norm = 1e-06


def from_behind(array, axis, by):
    devices = lax.axis_size(axis)
    pairs = [(i, i + by) for i in range(devices) if 0 <= i + by < devices]
    return lax.ppermute(array, axis, pairs)


def slot_table(chosen, num_experts):
    expert_range = jnp.arange(num_experts, dtype=jnp.int32)
    matched = (chosen[..., None] == expert_range).astype(jnp.int32)
    hit_table = jnp.sum(matched, axis=-2, dtype=jnp.int32)
    earlier = jnp.cumsum(hit_table, axis=-2, dtype=jnp.int32) - hit_table
    slot_index = jnp.sum(matched * earlier[..., None, :], axis=-1, dtype=jnp.int32)
    inside = chosen < num_experts
    return (slot_index, inside)


def place_mask(chosen, slot_index, inside, num_experts):
    flat_index = chosen * CAP + slot_index
    target = jnp.arange(num_experts * CAP, dtype=jnp.int32)
    return (flat_index[..., None] == target) & inside[..., None]


def moe_layer(rows, gain_row, gate_mat, up_mat, down_mat, chosen, weights_k):
    n_dev = lax.axis_size("expert")
    group_size = min(8, n_dev)
    num_experts = n_dev // group_size
    width_model = rows.shape[1]
    rows_float = rows.astype(jnp.float32)
    scale = lax.rsqrt(jnp.mean(rows_float * rows_float, axis=-1, keepdims=True) + eps_norm)
    normed = (rows_float * scale * gain_row).astype(jnp.bfloat16)
    slot_index, inside = slot_table(chosen, num_experts)
    placed = place_mask(chosen, slot_index, inside, num_experts)
    mask_any = jnp.any(placed, axis=1).astype(jnp.bfloat16)
    send_block = jnp.dot(mask_any.T, normed, preferred_element_type=jnp.float32).astype(
        jnp.bfloat16
    )
    send_block = send_block.reshape(num_experts, CAP, width_model)
    send_all = jnp.repeat(send_block, group_size, axis=0)
    received = lax.all_to_all(send_all, "expert", split_axis=0, concat_axis=0, tiled=True)
    rows_in = received.reshape(n_dev * CAP, width_model)
    gate_val = jnp.dot(rows_in, gate_mat, preferred_element_type=jnp.float32)
    up_val = jnp.dot(rows_in, up_mat, preferred_element_type=jnp.float32)
    hidden = (jax.nn.silu(gate_val) * up_val).astype(jnp.bfloat16)
    partial_value = jnp.dot(hidden, down_mat, preferred_element_type=jnp.float32).astype(
        jnp.bfloat16
    )
    returned = lax.all_to_all(
        partial_value.reshape(n_dev, CAP, width_model),
        "expert",
        split_axis=0,
        concat_axis=0,
        tiled=True,
    )
    expert_out = jnp.sum(
        returned.reshape(num_experts, group_size, CAP, width_model).astype(jnp.float32), axis=1
    )
    expert_out = expert_out.reshape(num_experts * CAP, width_model)
    weight_table = jnp.sum(jnp.where(placed, weights_k[:, :, None], 0.0), axis=1)
    routed_sum = jnp.dot(
        weight_table,
        expert_out,
        precision=lax.Precision.HIGHEST,
        preferred_element_type=jnp.float32,
    )
    return (rows_float + routed_sum).astype(jnp.bfloat16)


def shards(embedded, norm_gain, gate_proj, up_proj, down_proj, expert_ids, route_gates):
    n_section = lax.axis_size("section")
    section_pos = lax.axis_index("section")
    micro_count = expert_ids.shape[1]
    steps_total = micro_count + n_section - 1
    own_block = embedded[0]
    carry_rows = jnp.zeros_like(own_block)
    every_block = lax.all_gather(embedded, "section", axis=0, tiled=True)
    finished = jnp.zeros_like(every_block)
    for moment in range(steps_total):
        micro_pos = moment - section_pos
        clipped = jnp.clip(micro_pos, 0, micro_count - 1)
        chosen = lax.dynamic_index_in_dim(expert_ids[0], clipped, 0, keepdims=False)
        weights_k = lax.dynamic_index_in_dim(route_gates[0], clipped, 0, keepdims=False)
        if moment < micro_count:
            fresh_rows = every_block[moment]
        else:
            fresh_rows = jnp.zeros_like(own_block)
        layer_in = jnp.where(section_pos == 0, fresh_rows, carry_rows)
        layer_out = moe_layer(
            layer_in, norm_gain[0], gate_proj[0], up_proj[0], down_proj[0], chosen, weights_k
        )
        if moment >= n_section - 1:
            finished = finished.at[moment - n_section + 1].set(layer_out)
        if moment < steps_total - 1:
            carry_rows = from_behind(layer_out, "section", 1)
    spread = lax.all_to_all(finished, "section", split_axis=0, concat_axis=0, tiled=True)
    result = spread[n_section - 1]
    return result[None]


def solution(mesh):
    placed = (
        P("section", "expert", None),
        P("section", None),
        P("section", None, "expert"),
        P("section", None, "expert"),
        P("section", "expert", None),
        P("section", None, "expert", None),
        P("section", None, "expert", None),
    )
    return jax.shard_map(
        shards, mesh=mesh, in_specs=placed, out_specs=P("section", "expert", None), check_vma=False
    )
```

profile of v0, /device:TPU:6, one launch (start us, length us, event | category | flops | bytes accessed | tf_op | source)
XLA Modules:
  0.0 964.2 jit_solution(15735067081471994852)
XLA Ops:
  1.2 14.9 %all_gather.3 = bf16[4,16,7168]{2,1,0:T(8,128)(2,1)S(1)} all-gather(bf16[1,16,7168]{2,1,0:T(8,128)(2,1)} %param.15), channel_id=1, replica_groups=mesh['section'=4,'expert'=64] {'section'}, dimensions={0}, use_global_device_ids=true | all-gather | bytes 1146880 | tf_op jit(solution)/shard_map/all_gather | solution.py:86
  18.6 57.8 %all_to_all.75 = bf16[64,2,7168]{2,1,0:T(2,128)(2,1)} all-to-all(bf16[64,2,7168]{2,1,0:T(2,128)(2,1)S(1)} %bitcast.220), channel_id=1, replica_groups=mesh['section'=4,'expert'=64] {'expert'}, dimensions={0} | all-to-all | bytes 3670016 | tf_op jit(solution)/shard_map/all_to_all | solution.py:50
  76.3 4.1 reshape.520
  83.1 6.5 convolution_convert_fusion.6
  89.6 4.7 reshape.521
  94.4 5.5 all-to-all-start.1
  100.5 45.1 %all-to-all-done.1 = bf16[64,2,7168]{2,1,0:T(2,128)(2,1)S(1)} async-done(((bf16[64,2,7168]{2,1,0:T(2,128)(2,1)}), bf16[64,2,7168]{2,1,0:T(2,128)(2,1)S(1)}, u32[]{:S(2)}, u32[]{:S(2)}) %all-to-all-start.1) | async-done | bytes 1835040 | tf_op jit(solution)/shard_map/all_to_all | solution.py:58
  150.1 5.9 collective-permute-done
  157.6 52.1 %all_to_all.76 = bf16[64,2,7168]{2,1,0:T(2,128)(2,1)} all-to-all(bf16[64,2,7168]{2,1,0:T(2,128)(2,1)S(1)} %bitcast.221), channel_id=1, replica_groups=mesh['section'=4,'expert'=64] {'expert'}, dimensions={0} | all-to-all | bytes 3670016 | tf_op jit(solution)/shard_map/all_to_all | solution.py:50
  209.7 4.1 reshape.525
  216.5 6.5 convolution_convert_fusion.5
  223.0 4.7 reshape.526
  227.7 5.3 all-to-all-start.3
  233.3 45.5 %all-to-all-done.3 = bf16[64,2,7168]{2,1,0:T(2,128)(2,1)S(1)} async-done(((bf16[64,2,7168]{2,1,0:T(2,128)(2,1)}), bf16[64,2,7168]{2,1,0:T(2,128)(2,1)S(1)}, u32[]{:S(2)}, u32[]{:S(2)}) %all-to-all-start.3) | async-done | bytes 1835040 | tf_op jit(solution)/shard_map/all_to_all | solution.py:58
  282.9 6.4 collective-permute-done.1
  290.8 52.3 %all_to_all.77 = bf16[64,2,7168]{2,1,0:T(2,128)(2,1)} all-to-all(bf16[64,2,7168]{2,1,0:T(2,128)(2,1)S(1)} %bitcast.222), channel_id=1, replica_groups=mesh['section'=4,'expert'=64] {'expert'}, dimensions={0} | all-to-all | bytes 3670016 | tf_op jit(solution)/shard_map/all_to_all | solution.py:50
  343.1 4.1 reshape.530
  349.9 6.5 convolution_convert_fusion.4
  356.4 4.7 reshape.531
  361.2 5.3 all-to-all-start.5
  367.1 45.1 %all-to-all-done.5 = bf16[64,2,7168]{2,1,0:T(2,128)(2,1)S(1)} async-done(((bf16[64,2,7168]{2,1,0:T(2,128)(2,1)}), bf16[64,2,7168]{2,1,0:T(2,128)(2,1)S(1)}, u32[]{:S(2)}, u32[]{:S(2)}) %all-to-all-start.5) | async-done | bytes 1835040 | tf_op jit(solution)/shard_map/all_to_all | solution.py:58
  416.3 6.4 collective-permute-done.2
  424.3 52.3 %all_to_all.78 = bf16[64,2,7168]{2,1,0:T(2,128)(2,1)} all-to-all(bf16[64,2,7168]{2,1,0:T(2,128)(2,1)S(1)} %bitcast.223), channel_id=1, replica_groups=mesh['section'=4,'expert'=64] {'expert'}, dimensions={0} | all-to-all | bytes 3670016 | tf_op jit(solution)/shard_map/all_to_all | solution.py:50
  483.3 6.5 convolution_convert_fusion.3
  489.9 4.7 reshape.536
  494.6 5.3 all-to-all-start.7
  500.2 45.5 %all-to-all-done.7 = bf16[64,2,7168]{2,1,0:T(2,128)(2,1)S(1)} async-done(((bf16[64,2,7168]{2,1,0:T(2,128)(2,1)}), bf16[64,2,7168]{2,1,0:T(2,128)(2,1)S(1)}, u32[]{:S(2)}, u32[]{:S(2)}) %all-to-all-start.7) | async-done | bytes 1835040 | tf_op jit(solution)/shard_map/all_to_all | solution.py:58
  549.8 6.4 collective-permute-done.3
  557.7 52.5 %all_to_all.79 = bf16[64,2,7168]{2,1,0:T(2,128)(2,1)} all-to-all(bf16[64,2,7168]{2,1,0:T(2,128)(2,1)S(1)} %bitcast.224), channel_id=1, replica_groups=mesh['section'=4,'expert'=64] {'expert'}, dimensions={0} | all-to-all | bytes 3670016 | tf_op jit(solution)/shard_map/all_to_all | solution.py:50
  616.9 6.5 convolution_convert_fusion.2
  623.5 4.7 reshape.542
  628.2 5.3 all-to-all-start.9
  634.3 45.0 %all-to-all-done.9 = bf16[64,2,7168]{2,1,0:T(2,128)(2,1)S(1)} async-done(((bf16[64,2,7168]{2,1,0:T(2,128)(2,1)}), bf16[64,2,7168]{2,1,0:T(2,128)(2,1)S(1)}, u32[]{:S(2)}, u32[]{:S(2)}) %all-to-all-start.9) | async-done | bytes 1835040 | tf_op jit(solution)/shard_map/all_to_all | solution.py:58
  683.4 6.4 collective-permute-done.4
  691.3 52.3 %all_to_all.80 = bf16[64,2,7168]{2,1,0:T(2,128)(2,1)} all-to-all(bf16[64,2,7168]{2,1,0:T(2,128)(2,1)S(1)} %bitcast.225), channel_id=1, replica_groups=mesh['section'=4,'expert'=64] {'expert'}, dimensions={0} | all-to-all | bytes 3670016 | tf_op jit(solution)/shard_map/all_to_all | solution.py:50
  743.6 4.1 reshape.547
  750.3 6.5 convolution_convert_fusion.1
  756.9 4.7 reshape.548
  761.6 5.3 all-to-all-start.11
  767.2 45.5 %all-to-all-done.11 = bf16[64,2,7168]{2,1,0:T(2,128)(2,1)S(1)} async-done(((bf16[64,2,7168]{2,1,0:T(2,128)(2,1)}), bf16[64,2,7168]{2,1,0:T(2,128)(2,1)S(1)}, u32[]{:S(2)}, u32[]{:S(2)}) %all-to-all-start.11) | async-done | bytes 1835040 | tf_op jit(solution)/shard_map/all_to_all | solution.py:58
  816.8 6.4 collective-permute-done.5
  824.7 52.3 %all_to_all.81 = bf16[64,2,7168]{2,1,0:T(2,128)(2,1)} all-to-all(bf16[64,2,7168]{2,1,0:T(2,128)(2,1)S(1)} %bitcast.226), channel_id=1, replica_groups=mesh['section'=4,'expert'=64] {'expert'}, dimensions={0} | all-to-all | bytes 3670016 | tf_op jit(solution)/shard_map/all_to_all | solution.py:50
  877.0 4.1 reshape.553
  883.8 6.5 convolution_convert_fusion
  890.3 4.7 reshape.554
  895.1 5.3 all-to-all-start.13
  900.6 45.5 %all-to-all-done.13 = bf16[64,2,7168]{2,1,0:T(2,128)(2,1)S(1)} async-done(((bf16[64,2,7168]{2,1,0:T(2,128)(2,1)}), bf16[64,2,7168]{2,1,0:T(2,128)(2,1)S(1)}, u32[]{:S(2)}, u32[]{:S(2)}) %all-to-all-start.13) | async-done | bytes 1835040 | tf_op jit(solution)/shard_map/all_to_all | solution.py:58
  948.6 14.7 %all_to_all.82 = bf16[4,16,7168]{2,1,0:T(8,128)(2,1)S(1)} all-to-all(bf16[4,16,7168]{2,1,0:T(8,128)(2,1)S(1)} %fusion.8), channel_id=1, replica_groups=mesh['section'=4,'expert'=64] {'section'}, dimensions={0} | all-to-all | bytes 1835008 | tf_op jit(solution)/shard_map/all_to_all | solution.py:105
  (160 shorter events, 70.0 us)
Async XLA Ops:
  94.4 5.5 copy-start.1
  94.4 51.2 %all-to-all-start.1 = ((bf16[64,2,7168]{2,1,0:T(2,128)(2,1)}), bf16[64,2,7168]{2,1,0:T(2,128)(2,1)S(1)}, u32[]{:S(2)}, u32[]{:S(2)}) async-start(bf16[64,2,7168]{2,1,0:T(2,128)(2,1)} %reshape.521), calls=%async_computation.1 | async-start | bytes 3670016 | tf_op jit(solution)/shard_map/all_to_all | solution.py:58
  147.2 9.1 copy-start
  148.0 8.0 collective-permute-start
  227.7 51.1 %all-to-all-start.3 = ((bf16[64,2,7168]{2,1,0:T(2,128)(2,1)}), bf16[64,2,7168]{2,1,0:T(2,128)(2,1)S(1)}, u32[]{:S(2)}, u32[]{:S(2)}) async-start(bf16[64,2,7168]{2,1,0:T(2,128)(2,1)} %reshape.526), calls=%async_computation.3 | async-start | bytes 3670016 | tf_op jit(solution)/shard_map/all_to_all | solution.py:58
  281.3 8.0 collective-permute-start.1
  361.2 51.1 %all-to-all-start.5 = ((bf16[64,2,7168]{2,1,0:T(2,128)(2,1)}), bf16[64,2,7168]{2,1,0:T(2,128)(2,1)S(1)}, u32[]{:S(2)}, u32[]{:S(2)}) async-start(bf16[64,2,7168]{2,1,0:T(2,128)(2,1)} %reshape.531), calls=%async_computation.5 | async-start | bytes 3670016 | tf_op jit(solution)/shard_map/all_to_all | solution.py:58
  414.7 8.0 collective-permute-start.2
  494.6 51.1 %all-to-all-start.7 = ((bf16[64,2,7168]{2,1,0:T(2,128)(2,1)}), bf16[64,2,7168]{2,1,0:T(2,128)(2,1)S(1)}, u32[]{:S(2)}, u32[]{:S(2)}) async-start(bf16[64,2,7168]{2,1,0:T(2,128)(2,1)} %reshape.536), calls=%async_computation.7 | async-start | bytes 3670016 | tf_op jit(solution)/shard_map/all_to_all | solution.py:58
  548.2 8.0 collective-permute-start.3
  628.2 51.1 %all-to-all-start.9 = ((bf16[64,2,7168]{2,1,0:T(2,128)(2,1)}), bf16[64,2,7168]{2,1,0:T(2,128)(2,1)S(1)}, u32[]{:S(2)}, u32[]{:S(2)}) async-start(bf16[64,2,7168]{2,1,0:T(2,128)(2,1)} %reshape.542), calls=%async_computation.9 | async-start | bytes 3670016 | tf_op jit(solution)/shard_map/all_to_all | solution.py:58
  681.8 8.0 collective-permute-start.4
  761.6 51.1 %all-to-all-start.11 = ((bf16[64,2,7168]{2,1,0:T(2,128)(2,1)}), bf16[64,2,7168]{2,1,0:T(2,128)(2,1)S(1)}, u32[]{:S(2)}, u32[]{:S(2)}) async-start(bf16[64,2,7168]{2,1,0:T(2,128)(2,1)} %reshape.548), calls=%async_computation.11 | async-start | bytes 3670016 | tf_op jit(solution)/shard_map/all_to_all | solution.py:58
  815.2 8.0 collective-permute-start.5
  895.1 51.1 %all-to-all-start.13 = ((bf16[64,2,7168]{2,1,0:T(2,128)(2,1)}), bf16[64,2,7168]{2,1,0:T(2,128)(2,1)S(1)}, u32[]{:S(2)}, u32[]{:S(2)}) async-start(bf16[64,2,7168]{2,1,0:T(2,128)(2,1)} %reshape.554), calls=%async_computation.13 | async-start | bytes 3670016 | tf_op jit(solution)/shard_map/all_to_all | solution.py:58
where the time goes:
time: 976 us; the launch traced here: 964 us
  blocking collectives  401 us (41%)
  waiting for transfers between devices  355 us (36%)
  local copies, waits for them, and re-layouts  74.5 us (8%)
  matrix products  70.9 us (7%)
  starting transfers between devices  45.7 us (5%)
  other arithmetic  15.7 us (2%)
    all_to_all x7, blocking collectives, moe_layer(): lax.all_to_all(send_all, 'expert', split_axis=0, concat_axis=0, tiled=True)  372 us
    all_to_all x7, waiting for transfers between devices, moe_layer(): lax.all_to_all(partial_value.reshape(n_dev, CAP, width_model), 'expert',...  317 us
    dot_general x7, matrix products, moe_layer(): jnp.dot(hidden, down_mat, preferred_element_type=jnp.float32)  45.8 us
    ppermute x6, waiting for transfers between devices, from_behind(): return lax.ppermute(array, axis, pairs)  38 us
    all_to_all x7, starting transfers between devices, moe_layer(): lax.all_to_all(partial_value.reshape(n_dev, CAP, width_model), 'expert',...  37.5 us
    reshape x7, local copies, waits for them, and re-layouts, moe_layer(): partial_value.reshape(n_dev, CAP, width_model)  33.2 us
    reshape x7, local copies, waits for them, and re-layouts, moe_layer(): rows_in = received.reshape(n_dev * CAP, width_model)  28.4 us
  transfers between devices with their start and end apart: 13, of which 13 were waited for; matrix products, arithmetic and copies ran while one was open for 0% of the time, Pallas kernels for 0%

commit v1 on v0

v1 whole, which is shorter than its diff:
```python
import functools

import jax
import jax.numpy as jnp
from jax import lax
from jax.experimental import pallas as pl
from jax.experimental.pallas import tpu as pltpu
from jax.sharding import PartitionSpec as P

MESH = pl.DeviceIdType.MESH
F32 = jnp.float32
BF16 = jnp.bfloat16

D = 7168
J = 8
W = D // J
HID = 256
MB = 4
TOK = 16
CHUNKS = ((0, 512), (512, 384))
EPS = 1e-06
Z_ORDER = (4, 3, 5, 2, 6, 1, 7)


class Refs:
    pass


def scratch_plan():
    dma = pltpu.SemaphoreType.DMA
    plan = [
        ("wg", pltpu.VMEM((D, HID), BF16)),
        ("wu", pltpu.VMEM((D, HID), BF16)),
        ("wd", pltpu.VMEM((HID, D), BF16)),
        ("wsem", dma((3,))),
        ("hb", pltpu.VMEM((128, HID), BF16)),
        ("pm", pltpu.VMEM((MB, 128, 128), BF16)),
        ("cm", pltpu.VMEM((MB + 1, 2, 128, 128), BF16)),
        ("qm", pltpu.VMEM((128, 128), BF16)),
        ("rp", pltpu.VMEM((8, 128), F32)),
        ("rf", pltpu.VMEM((8, 128), F32)),
        ("rp_s", dma),
        ("rf_s", dma((4,))),
        ("rp_r", dma),
        ("rf_r", dma),
        ("xr", pltpu.VMEM((MB + 1, 128, W), BF16)),
        ("xr_r", dma((MB + 1,))),
        ("xi_s", dma),
        ("xc", pltpu.VMEM((MB, 128, W), BF16)),
        ("xc_s", dma((MB,))),
    ]
    for i, (_, w) in enumerate(CHUNKS):
        plan += [
            (f"sz{i}", pltpu.VMEM((MB, 128, w), BF16)),
            (f"rz{i}", pltpu.VMEM((MB, 128, w), BF16)),
            (f"xb{i}", pltpu.VMEM((MB, J, 128, w), BF16)),
            (f"pb{i}", pltpu.VMEM((MB, J, 128, w), BF16)),
            (f"cr{i}", pltpu.VMEM((MB, J, 64, w), BF16)),
            (f"sb{i}", pltpu.VMEM((MB, J, 64, w), BF16)),
            (f"rl{i}", pltpu.VMEM((MB, J // 2, 16, w), BF16)),
            (f"rr{i}", pltpu.VMEM((MB, J // 2, 16, w), BF16)),
            (f"s2{i}", pltpu.VMEM((MB, J, 16, w), BF16)),
            (f"fl{i}", pltpu.VMEM((MB, J, 16, w), BF16)),
            (f"fr{i}", pltpu.VMEM((MB, J, 16, w), BF16)),
            (f"zs{i}", pltpu.VMEM((MB, 128, w), BF16)),
            (f"rt{i}", pltpu.VMEM((MB + 1, 128, w), BF16)),
        ]
        for name in ("szs", "rzr", "ags", "agl", "agr", "afl", "afr", "agc", "rss", "crr", "rlr", "rrr", "flr", "frr", "zss"):
            plan.append((f"{name}{i}", dma((MB,))))
        plan.append((f"rtr{i}", dma((MB + 1,))))
    return plan


PLAN = scratch_plan()


def iotas():
    return (
        lax.broadcasted_iota(jnp.int32, (128, 128), 0),
        lax.broadcasted_iota(jnp.int32, (128, 128), 1),
    )


def dot(a, b):
    return jnp.dot(a, b, preferred_element_type=F32)


def dot_nt(a, b):
    return lax.dot_general(a, b, (((1,), (1,)), ((), ())), preferred_element_type=F32)


def one_hot(cond):
    return jnp.where(cond, 1.0, 0.0).astype(BF16)


def dispatch_matrix(ids_row):
    r, l = iotas()
    named = one_hot(ids_row == (r >> 4).astype(F32))
    same = one_hot((r >> 3) == (l >> 3))
    before = one_hot((r >> 3) < (l >> 3))
    hit = dot(named, same)
    prior = dot(named, before)
    keep = (hit > 0.5) & (prior == (r & 1).astype(F32)) & (((r >> 1) & 7) == (l & 7))
    return one_hot(keep)


def combine_matrices(ids_row, gate_row):
    r, l = iotas()
    hits = jnp.where(ids_row == (r >> 4).astype(F32), 1.0, 0.0)
    named = hits.astype(BF16)
    gated = hits * gate_row
    high = gated.astype(BF16)
    low = (gated - high.astype(F32)).astype(BF16)
    same = one_hot((r >> 3) == (l >> 3))
    before = one_hot((l >> 3) < (r >> 3))
    hit = dot_nt(same, named)
    prior = dot_nt(before, named)
    keep = (hit > 0.5) & (prior == (l & 1).astype(F32)) & (((l >> 1) & 7) == (r & 7))
    return (
        jnp.where(keep, dot_nt(same, high), 0.0).astype(BF16),
        jnp.where(keep, dot_nt(same, low), 0.0).astype(BF16),
    )


def swap_matrix():
    r, l = iotas()
    return one_hot(
        ((r >> 4) == ((l >> 1) & 7)) & (((r >> 1) & 7) == (l >> 4)) & ((r & 1) == (l & 1))
    )


def kernel(x_ref, gain_ref, route_ref, wg_hbm, wu_hbm, wd_hbm, o_ref, *scratch):
    R = Refs()
    for (name, _), ref in zip(PLAN, scratch):
        setattr(R, name, ref)
    get = lambda name, ch: getattr(R, f"{name}{ch}")

    s = lax.axis_index("section")
    ex = lax.axis_index("expert")
    z, y, c = ex // 8, (ex // 2) % 4, ex % 2
    last = s // 3

    def at(z2, y2, c2):
        return (z2 * 4 + y2) * 2 + c2

    up_y, down_y = (s, at(z, (y + 1) % 4, c)), (s, at(z, (y + 3) % 4, c))
    partner = (s, at(z, y, 1 - c))

    def rows(c2, y2):
        return pl.ds(pl.multiple_of((c2 * 4 + y2) * 16, 16), 16)

    def yrows(y2):
        return pl.ds(pl.multiple_of(y2 * 16, 16), 16)

    def half(c2):
        return pl.ds(pl.multiple_of(c2 * 64, 64), 64)

    def send(src, dst, ssem, rsem, dev):
        pltpu.make_async_remote_copy(
            src_ref=src, dst_ref=dst, send_sem=ssem, recv_sem=rsem, device_id=dev, device_id_type=MESH
        ).start()

    def wait(ref, sem):
        pltpu.make_async_copy(ref, ref, sem).wait()

    weights = [
        pltpu.make_async_copy(src, dst, R.wsem.at[i])
        for i, (src, dst) in enumerate(((wg_hbm, R.wg), (wu_hbm, R.wu), (wd_hbm, R.wd)))
    ]
    for copy in weights:
        copy.start()

    barrier = pltpu.get_barrier_semaphore()
    place = s * 8 + z

    def greet(d, carry):
        other = (place + d) % 32
        pl.semaphore_signal(barrier, inc=1, device_id=(other // 8, at(other % 8, y, c)), device_id_type=MESH)
        return carry

    lax.fori_loop(1, 32, greet, 0)
    for dev in (up_y, down_y, partner):
        pl.semaphore_signal(barrier, inc=1, device_id=dev, device_id_type=MESH)

    R.qm[...] = swap_matrix()

    def prepare(m, carry):
        R.pm[m] = dispatch_matrix(route_ref[pl.ds(m, 1), :])
        return carry

    lax.fori_loop(0, MB, prepare, 0)
    pl.semaphore_wait(barrier, 34)

    @pl.when(s < 3)
    def _():
        send(route_ref, R.rp, R.rp_s, R.rp_r, (s + 1, ex))

    @pl.when(s == 3)
    def _():
        for t in range(3):
            send(route_ref, R.rf, R.rf_s.at[t], R.rf_r, (t, ex))
        pltpu.make_async_copy(route_ref, R.rf, R.rf_r).start()

    @pl.when(s > 0)
    def _():
        send(x_ref, R.xr.at[s], R.xi_s, R.xr_r.at[s], (0, ex))

    @pl.when(s == 0)
    def _():
        pltpu.make_async_copy(x_ref, R.xr.at[0], R.xr_r.at[0]).start()

    @pl.when(s > 0)
    def _():
        wait(R.rp, R.rp_r)

        def build(m, carry):
            high, low = combine_matrices(R.rp[pl.ds(m, 1), :], R.rp[pl.ds(m + 4, 1), :])
            R.cm[m, 0] = high
            R.cm[m, 1] = low
            return carry

        lax.fori_loop(0, MB, build, 0)

    def combined(slot, ch, lane, w):
        got = get("rt", ch)[slot]
        added = dot(R.cm[slot, 0], got) + dot(R.cm[slot, 1], got)
        return (R.xr[slot, :, lane : lane + w].astype(F32) + added).astype(BF16)

    def target(m):
        return (1 - last) * (s + 1) + last * m, (1 - last) * m + last * 4

    def stage_a(m):
        wait(R.xr.at[m], R.xr_r.at[m])

        @pl.when(s == 0)
        def _():
            R.xc[m] = R.xr[m]

        @pl.when(s > 0)
        def _():
            for ch, (lane, w) in enumerate(CHUNKS):
                wait(get("rt", ch).at[m], get("rtr", ch).at[m])
                R.xc[m, :, lane : lane + w] = combined(m, ch, lane, w)

        total = jnp.zeros((TOK, J, 1), F32)
        for lane, w in CHUNKS:
            part = R.xc[m, :, lane : lane + w].astype(F32).reshape(TOK, J, w)
            total = total + jnp.sum(part * part, axis=2, keepdims=True)
        scale = lax.rsqrt(jnp.sum(total, axis=1, keepdims=True) * (1.0 / D) + EPS)
        for ch, (lane, w) in enumerate(CHUNKS):
            part = R.xc[m, :, lane : lane + w].astype(F32).reshape(TOK, J, w)
            normed = part * scale * gain_ref[:, lane : lane + w][None]
            normed = normed.reshape(128, w).astype(BF16)
            sz, rz = get("sz", ch), get("rz", ch)
            sz[m] = dot(R.pm[m], normed).astype(BF16)
            mine = pl.ds(pl.multiple_of(z * 16, 16), 16)
            for d in Z_ORDER:
                z2 = (z + d) % 8
                send(
                    sz.at[m, pl.ds(pl.multiple_of(z2 * 16, 16), 16)],
                    rz.at[m, mine],
                    get("szs", ch).at[m],
                    get("rzr", ch).at[m],
                    (s, at(z2, y, c)),
                )
            pltpu.make_async_copy(sz.at[m, mine], rz.at[m, mine], get("rzr", ch).at[m]).start()
        sd, slot = target(m)

        @pl.when(sd != s)
        def _():
            send(R.xc.at[m], R.xr.at[slot], R.xc_s.at[m], R.xr_r.at[slot], (sd, ex))

        @pl.when(sd == s)
        def _():
            pltpu.make_async_copy(R.xc.at[m], R.xr.at[slot], R.xr_r.at[slot]).start()

    def stage_b(m):
        mine = rows(c, y)
        for ch, (_, w) in enumerate(CHUNKS):
            rz, xb = get("rz", ch), get("xb", ch)
            wait(rz.at[m], get("rzr", ch).at[m])
            xb[m, :, mine, :] = dot(R.qm[...], rz[m]).astype(BF16).reshape(J, 16, w)
            block = xb.at[m, :, mine]
            ssem = get("ags", ch).at[m]
            send(block, block, ssem, get("agl", ch).at[m], up_y)
            send(block, block, ssem, get("agr", ch).at[m], down_y)
            send(block, block, ssem, get("agc", ch).at[m], partner)

    def stage_c(m):
        left, right, far = rows(c, (y + 3) % 4), rows(c, (y + 1) % 4), rows(c, (y + 2) % 4)
        low, high = pl.ds(0, J // 2), pl.ds(J // 2, J // 2)
        for ch in range(len(CHUNKS)):
            xb, ssem, csem = get("xb", ch), get("ags", ch).at[m], get("agc", ch).at[m]
            block = xb.at[m, :, left]
            wait(block, get("agl", ch).at[m])
            piece = xb.at[m, low, left]
            send(piece, piece, ssem, get("afl", ch).at[m], up_y)
            send(block, block, ssem, csem, partner)
            block = xb.at[m, :, right]
            wait(block, get("agr", ch).at[m])
            piece = xb.at[m, high, right]
            send(piece, piece, ssem, get("afr", ch).at[m], down_y)
            send(block, block, ssem, csem, partner)
        for ch in range(len(CHUNKS)):
            xb, ssem, csem = get("xb", ch), get("ags", ch).at[m], get("agc", ch).at[m]
            wait(xb.at[m, low, far], get("afl", ch).at[m])
            wait(xb.at[m, high, far], get("afr", ch).at[m])
            block = xb.at[m, :, far]
            send(block, block, ssem, csem, partner)

    def stage_d(m):
        @pl.when(m == 0)
        def _():
            for copy in weights:
                copy.wait()

        gate = jnp.zeros((128, HID), F32)
        up = jnp.zeros((128, HID), F32)
        for ch, (lane, w) in enumerate(CHUNKS):
            xb = get("xb", ch)
            wait(xb.at[m, pl.ds(0, 4)], get("agc", ch).at[m])
            for j in range(J):
                value = xb[m, j]
                gate = gate + dot(value, R.wg[j * W + lane : j * W + lane + w, :])
                up = up + dot(value, R.wu[j * W + lane : j * W + lane + w, :])
        R.hb[...] = (gate * jax.nn.sigmoid(gate) * up).astype(BF16)
        for ch, (lane, w) in enumerate(CHUNKS):
            pb = get("pb", ch)
            for j in range(J):
                pb[m, j] = dot(R.hb[...], R.wd[:, j * W + lane : j * W + lane + w]).astype(BF16)
            send(pb.at[m, :, half(1 - c)], get("cr", ch).at[m], get("rss", ch).at[m], get("crr", ch).at[m], partner)

    def stage_e(m):
        h = J // 2
        low, high = pl.ds(0, h), pl.ds(h, h)
        for ch in range(len(CHUNKS)):
            cr, sb, ssem = get("cr", ch), get("sb", ch), get("rss", ch).at[m]
            wait(cr.at[m], get("crr", ch).at[m])
            for j in range(J):
                own = get("pb", ch)[m, j, half(c), :].astype(F32)
                sb[m, j] = (own + cr[m, j].astype(F32)).astype(BF16)
            far = yrows((y + 2) % 4)
            send(sb.at[m, low, far], get("rl", ch).at[m], ssem, get("rlr", ch).at[m], up_y)
            send(sb.at[m, high, far], get("rr", ch).at[m], ssem, get("rrr", ch).at[m], down_y)
            send(sb.at[m, high, yrows((y + 1) % 4)], get("fl", ch).at[m, high], ssem, get("flr", ch).at[m], up_y)
            send(sb.at[m, low, yrows((y + 3) % 4)], get("fr", ch).at[m, low], ssem, get("frr", ch).at[m], down_y)

    def stage_f(m):
        h = J // 2
        low, high = pl.ds(0, h), pl.ds(h, h)
        for ch in range(len(CHUNKS)):
            sb, s2, ssem = get("sb", ch), get("s2", ch), get("rss", ch).at[m]
            wait(get("rl", ch).at[m], get("rlr", ch).at[m])
            s2[m, low] = (sb[m, low, yrows((y + 1) % 4), :].astype(F32) + get("rl", ch)[m].astype(F32)).astype(BF16)
            send(s2.at[m, low], get("fl", ch).at[m, low], ssem, get("flr", ch).at[m], up_y)
            wait(get("rr", ch).at[m], get("rrr", ch).at[m])
            s2[m, high] = (sb[m, high, yrows((y + 3) % 4), :].astype(F32) + get("rr", ch)[m].astype(F32)).astype(BF16)
            send(s2.at[m, high], get("fr", ch).at[m, high], ssem, get("frr", ch).at[m], down_y)

    def stage_g(m):
        sd, slot = target(m)
        mine = pl.ds(pl.multiple_of(z * 16, 16), 16)
        for ch, (_, w) in enumerate(CHUNKS):
            fl, fr, zs, rt = get("fl", ch), get("fr", ch), get("zs", ch), get("rt", ch)
            wait(fl.at[m], get("flr", ch).at[m])
            wait(fr.at[m], get("frr", ch).at[m])
            total = get("sb", ch)[m, :, yrows(y), :].astype(F32) + fl[m].astype(F32) + fr[m].astype(F32)
            zs[m] = dot(R.qm[...], total.astype(BF16).reshape(128, w)).astype(BF16)
            for d in Z_ORDER:
                z2 = (z + d) % 8
                send(
                    zs.at[m, pl.ds(pl.multiple_of(z2 * 16, 16), 16)],
                    rt.at[slot, mine],
                    get("zss", ch).at[m],
                    get("rtr", ch).at[slot],
                    (sd, at(z2, y, c)),
                )

            @pl.when(sd != s)
            def _():
                send(zs.at[m, mine], rt.at[slot, mine], get("zss", ch).at[m], get("rtr", ch).at[slot], (sd, ex))

            @pl.when(sd == s)
            def _():
                pltpu.make_async_copy(zs.at[m, mine], rt.at[slot, mine], get("rtr", ch).at[slot]).start()

    def turn(i, carry):
        back, front = i >= 1, i < MB

        def on(cond, stage, m):
            pl.when(cond)(functools.partial(stage, m))

        on(back, stage_d, i - 1)
        on(front, stage_a, i)
        on(back, stage_e, i - 1)
        on(front, stage_b, i)
        on(back, stage_f, i - 1)
        on(front, stage_c, i)
        on(back, stage_g, i - 1)
        return carry

    lax.fori_loop(0, MB + 1, turn, 0)

    wait(R.rf, R.rf_r)
    high, low = combine_matrices(R.rf[pl.ds(s, 1), :], R.rf[pl.ds(s + 4, 1), :])
    R.cm[MB, 0] = high
    R.cm[MB, 1] = low
    wait(R.xr.at[MB], R.xr_r.at[MB])
    for ch, (lane, w) in enumerate(CHUNKS):
        wait(get("rt", ch).at[MB], get("rtr", ch).at[MB])
        o_ref[:, lane : lane + w] = combined(MB, ch, lane, w)

    @pl.when(s < 3)
    def _():
        wait(R.rp, R.rp_s)

    @pl.when(s == 3)
    def _():
        for t in range(3):
            wait(R.rf, R.rf_s.at[t])

    @pl.when(s > 0)
    def _():
        wait(x_ref, R.xi_s)

    def drain(m, carry):
        sd, _ = target(m)

        @pl.when(sd != s)
        def _():
            wait(R.xc.at[m], R.xc_s.at[m])

        for ch in range(len(CHUNKS)):
            wait(get("sz", ch).at[m, pl.ds(0, 112)], get("szs", ch).at[m])
            wait(get("xb", ch).at[m, pl.ds(0, 7)], get("ags", ch).at[m])
            wait(get("pb", ch).at[m, pl.ds(0, 7)], get("rss", ch).at[m])

            @pl.when(sd != s)
            def _():
                wait(get("zs", ch).at[m], get("zss", ch).at[m])

            @pl.when(sd == s)
            def _():
                wait(get("zs", ch).at[m, pl.ds(0, 112)], get("zss", ch).at[m])

        return carry

    lax.fori_loop(0, MB, drain, 0)


def shards(embedded, norm_gain, gate_proj, up_proj, down_proj, expert_ids, route_gates):
    rows = embedded.reshape(128, W)
    gain = norm_gain.reshape(J, W)
    route = jnp.concatenate(
        [expert_ids.reshape(MB, 128).astype(F32), route_gates.reshape(MB, 128)], axis=0
    )
    vmem, hbm = pl.BlockSpec(memory_space=pltpu.VMEM), pl.BlockSpec(memory_space=pl.ANY)
    out = pl.pallas_call(
        kernel,
        out_shape=jax.ShapeDtypeStruct((128, W), BF16),
        in_specs=[vmem, vmem, vmem, hbm, hbm, hbm],
        out_specs=vmem,
        scratch_shapes=[shape for _, shape in PLAN],
        compiler_params=pltpu.CompilerParams(
            collective_id=0, has_side_effects=True, vmem_limit_bytes=60 * 1024 * 1024
        ),
        name="expert_sections",
    )(rows, gain, route, gate_proj[0], up_proj[0], down_proj[0])
    return out.reshape(1, TOK, D)


def solution(mesh):
    placed = (
        P("section", "expert", None),
        P("section", None),
        P("section", None, "expert"),
        P("section", None, "expert"),
        P("section", "expert", None),
        P("section", None, "expert", None),
        P("section", None, "expert", None),
    )
    return jax.shard_map(
        shards, mesh=mesh, in_specs=placed, out_specs=P("section", "expert", None), check_vma=False
    )
```

time: 976 us -> 266 us (0.27); the launches traced: 964 us -> 266 us
  blocking collectives: 401 us -> 0 us
  waiting for transfers between devices: 355 us -> 0 us
  Pallas kernels: 0 us -> 257 us
  matrix products: 70.9 us -> 0 us
  local copies, waits for them, and re-layouts: 74.5 us -> 5.64 us
  starting transfers between devices: 45.7 us -> 0 us
  other arithmetic: 15.7 us -> 2.78 us
    all_to_all x8 -> x0, blocking collectives: 386 us -> none  [the longest x7 372 us: moe_layer(): lax.all_to_all(send_all, 'expert', split_axis=0, concat_axis=0, tiled=True)]
    all_to_all x7 -> x0, waiting for transfers between devices: 317 us -> none  [moe_layer(): lax.all_to_all(partial_value.reshape(n_dev, CAP, width_model), 'expert',...]
    pallas_call x0 -> x1, Pallas kernels: none -> 257 us  [shards(): pl.pallas_call(kernel, out_shape=jax.ShapeDtypeStruct((128, W), BF16), in...]
    dot_general x28 -> x0, matrix products: 70.9 us -> none  [the longest x7 45.8 us: moe_layer(): jnp.dot(hidden, down_mat, preferred_element_type=jnp.float32)]
    reshape x28 -> x4, local copies, waits for them, and re-layouts: 64.4 us -> 4.17 us  [the longest x1 1.73 us: shards(): return out.reshape(1, TOK, D)]
    ppermute x6 -> x0, waiting for transfers between devices: 38 us -> none  [from_behind(): return lax.ppermute(array, axis, pairs)]
    all_to_all x7 -> x0, starting transfers between devices: 37.5 us -> none  [moe_layer(): lax.all_to_all(partial_value.reshape(n_dev, CAP, width_model), 'expert',...]
    all_gather x1 -> x0, blocking collectives: 14.9 us -> none  [shards(): every_block = lax.all_gather(embedded, 'section', axis=0, tiled=True)]
  transfers between devices with their start and end apart: 13 -> 0, of which waited for: 13 -> 0; matrix products, arithmetic and copies ran while one was open for 0% -> 0% of each run, Pallas kernels for 0% -> 0%
where the time goes in v1:
time: 266 us
  Pallas kernels  257 us (97%)
  local copies, waits for them, and re-layouts  5.64 us (2%)
  other arithmetic  2.78 us (1%)
    pallas_call x1, Pallas kernels, shards(): pl.pallas_call(kernel, out_shape=jax.ShapeDtypeStruct((128, W), BF16), in...  257 us

profile of v1, /device:TPU:6, one launch (start us, length us, event | category | flops | bytes accessed | tf_op | source)
XLA Modules:
  0.0 265.8 jit_solution(16079470055462000983)
XLA Ops:
  0.0 0.7 convert_element_type.6
  0.7 0.1 copy.10
  0.8 0.1 convert_element_type.7
  0.9 0.5 broadcast.3
  1.4 1.5 reduce.3
  2.9 0.6 reshape.15.gain_ref
  3.5 0.8 copy.11
  4.3 0.1 reshape.16
  4.4 0.6 pad_maximum_fusion.route_ref
  5.0 1.7 reshape.14.x_ref
  6.7 257.3 %expert_sections.1 = bf16[128,896]{1,0:T(8,128)(2,1)} custom-call(bf16[128,896]{1,0:T(8,128)(2,1)} %reshape.14.x_ref, f32[8,896]{1,0:T(8,128)} %reshape.15.gain_ref, f32[8,128]{1,0:T(8,128)} %pad_maximum_fusion.route_ref, bf16[7168,256]{1,0:T(8,128)(2,1)} %bitcast.7, bf16[7168,256]{1,0:T(8,128)(2,1)} %bitcast.8, bf16[256,7168]{1,0:T(8,128)(2,1)} %bitcast.9), custom_call_target="tpu_custom_call" | custom-call | tf_op jit(solution)/shard_map/expert_sections/pallas_call | solution.py:458
  264.0 1.7 reshape.17

commit v2 on v1

--- a/solution.py
+++ b/solution.py
@@ -37,12 +37,14 @@
         ("pm", pltpu.VMEM((MB, 128, 128), BF16)),
         ("cm", pltpu.VMEM((MB + 1, 2, 128, 128), BF16)),
         ("qm", pltpu.VMEM((128, 128), BF16)),
-        ("rp", pltpu.VMEM((8, 128), F32)),
-        ("rf", pltpu.VMEM((8, 128), F32)),
-        ("rp_s", dma),
-        ("rf_s", dma((4,))),
-        ("rp_r", dma),
-        ("rf_r", dma),
+        ("rpi", pltpu.VMEM((MB, 8, TOK), jnp.int32)),
+        ("rpg", pltpu.VMEM((MB, 8, TOK), F32)),
+        ("rfi", pltpu.VMEM((8, TOK), jnp.int32)),
+        ("rfg", pltpu.VMEM((8, TOK), F32)),
+        ("rp_s", dma((2,))),
+        ("rf_s", dma((3, 2))),
+        ("rp_r", dma((2,))),
+        ("rf_r", dma((2,))),
         ("xr", pltpu.VMEM((MB + 1, 128, W), BF16)),
         ("xr_r", dma((MB + 1,))),
         ("xi_s", dma),
@@ -85,40 +87,43 @@
     return jnp.dot(a, b, preferred_element_type=F32)
 
 
-def dot_nt(a, b):
-    return lax.dot_general(a, b, (((1,), (1,)), ((), ())), preferred_element_type=F32)
-
-
 def one_hot(cond):
     return jnp.where(cond, 1.0, 0.0).astype(BF16)
 
 
-def dispatch_matrix(ids_row):
+def per_lane(a, pick):
+    token = lax.broadcasted_iota(jnp.int32, (TOK, 128), 0)
+    lane = lax.broadcasted_iota(jnp.int32, (TOK, 128), 1) & (TOK - 1)
+    return dot(a, one_hot(pick(token, lane)))
+
+
+def chosen(ids, values):
+    expert = lax.broadcasted_iota(jnp.int32, (128, TOK), 0) >> 4
+    total = jnp.zeros((128, TOK), F32)
+    for k in range(8):
+        total = total + jnp.where(ids[k : k + 1, :] == expert, values[k : k + 1, :], 0.0)
+    return total
+
+
+def placed(ids):
     r, l = iotas()
-    named = one_hot(ids_row == (r >> 4).astype(F32))
-    same = one_hot((r >> 3) == (l >> 3))
-    before = one_hot((r >> 3) < (l >> 3))
-    hit = dot(named, same)
-    prior = dot(named, before)
-    keep = (hit > 0.5) & (prior == (r & 1).astype(F32)) & (((r >> 1) & 7) == (l & 7))
-    return one_hot(keep)
-
-
-def combine_matrices(ids_row, gate_row):
-    r, l = iotas()
-    hits = jnp.where(ids_row == (r >> 4).astype(F32), 1.0, 0.0)
-    named = hits.astype(BF16)
-    gated = hits * gate_row
+    named = chosen(ids, jnp.ones((8, TOK), F32)).astype(BF16)
+    hit = per_lane(named, lambda t, lane: t == lane)
+    prior = per_lane(named, lambda t, lane: t < lane)
+    return (hit > 0.5) & (prior == (r & 1).astype(F32)) & (((r >> 1) & 7) == (l >> 4))
+
+
+def dispatch_matrix(ids):
+    return one_hot(placed(ids))
+
+
+def combine_matrices(ids, gates):
+    keep = placed(ids)
+    gated = chosen(ids, gates)
     high = gated.astype(BF16)
     low = (gated - high.astype(F32)).astype(BF16)
-    same = one_hot((r >> 3) == (l >> 3))
-    before = one_hot((l >> 3) < (r >> 3))
-    hit = dot_nt(same, named)
-    prior = dot_nt(before, named)
-    keep = (hit > 0.5) & (prior == (l & 1).astype(F32)) & (((l >> 1) & 7) == (r & 7))
-    return (
-        jnp.where(keep, dot_nt(same, high), 0.0).astype(BF16),
-        jnp.where(keep, dot_nt(same, low), 0.0).astype(BF16),
+    return tuple(
+        jnp.where(keep, per_lane(a, lambda t, lane: t == lane), 0.0).T.astype(BF16) for a in (high, low)
     )
 
 
@@ -129,7 +134,7 @@
     )
 
 
-def kernel(x_ref, gain_ref, route_ref, wg_hbm, wu_hbm, wd_hbm, o_ref, *scratch):
+def kernel(x_ref, gain_ref, ids_ref, gates_ref, wg_hbm, wu_hbm, wd_hbm, o_ref, *scratch):
     R = Refs()
     for (name, _), ref in zip(PLAN, scratch):
         setattr(R, name, ref)
@@ -185,7 +190,7 @@
     R.qm[...] = swap_matrix()
 
     def prepare(m, carry):
-        R.pm[m] = dispatch_matrix(route_ref[pl.ds(m, 1), :])
+        R.pm[m] = dispatch_matrix(ids_ref[m])
         return carry
 
     lax.fori_loop(0, MB, prepare, 0)
@@ -193,28 +198,34 @@
 
     @pl.when(s < 3)
     def _():
-        send(route_ref, R.rp, R.rp_s, R.rp_r, (s + 1, ex))
+        send(ids_ref, R.rpi, R.rp_s.at[0], R.rp_r.at[0], (s + 1, ex))
+        send(gates_ref, R.rpg, R.rp_s.at[1], R.rp_r.at[1], (s + 1, ex))
 
     @pl.when(s == 3)
     def _():
         for t in range(3):
-            send(route_ref, R.rf, R.rf_s.at[t], R.rf_r, (t, ex))
-        pltpu.make_async_copy(route_ref, R.rf, R.rf_r).start()
+            send(ids_ref.at[t], R.rfi, R.rf_s.at[t, 0], R.rf_r.at[0], (t, ex))
+            send(gates_ref.at[t], R.rfg, R.rf_s.at[t, 1], R.rf_r.at[1], (t, ex))
+        pltpu.make_async_copy(ids_ref.at[3], R.rfi, R.rf_r.at[0]).start()
+        pltpu.make_async_copy(gates_ref.at[3], R.rfg, R.rf_r.at[1]).start()
 
     @pl.when(s > 0)
     def _():
-        send(x_ref, R.xr.at[s], R.xi_s, R.xr_r.at[s], (0, ex))
+        for j in range(J):
+            send(x_ref.at[:, pl.ds(j * W, W)], R.xr.at[s, pl.ds(j * TOK, TOK)], R.xi_s, R.xr_r.at[s], (0, ex))
 
     @pl.when(s == 0)
     def _():
-        pltpu.make_async_copy(x_ref, R.xr.at[0], R.xr_r.at[0]).start()
+        for j in range(J):
+            pltpu.make_async_copy(x_ref.at[:, pl.ds(j * W, W)], R.xr.at[0, pl.ds(j * TOK, TOK)], R.xr_r.at[0]).start()
 
     @pl.when(s > 0)
     def _():
-        wait(R.rp, R.rp_r)
+        wait(R.rpi, R.rp_r.at[0])
+        wait(R.rpg, R.rp_r.at[1])
 
         def build(m, carry):
-            high, low = combine_matrices(R.rp[pl.ds(m, 1), :], R.rp[pl.ds(m + 4, 1), :])
+            high, low = combine_matrices(R.rpi[m], R.rpg[m])
             R.cm[m, 0] = high
             R.cm[m, 1] = low
             return carry
@@ -242,15 +253,17 @@
                 wait(get("rt", ch).at[m], get("rtr", ch).at[m])
                 R.xc[m, :, lane : lane + w] = combined(m, ch, lane, w)
 
-        total = jnp.zeros((TOK, J, 1), F32)
+        total = jnp.zeros((J, TOK, 1), F32)
         for lane, w in CHUNKS:
-            part = R.xc[m, :, lane : lane + w].astype(F32).reshape(TOK, J, w)
+            part = R.xc[m, :, lane : lane + w].astype(F32).reshape(J, TOK, w)
             total = total + jnp.sum(part * part, axis=2, keepdims=True)
-        scale = lax.rsqrt(jnp.sum(total, axis=1, keepdims=True) * (1.0 / D) + EPS)
+        scale = lax.rsqrt(jnp.sum(total, axis=0) * (1.0 / D) + EPS)
         for ch, (lane, w) in enumerate(CHUNKS):
-            part = R.xc[m, :, lane : lane + w].astype(F32).reshape(TOK, J, w)
-            normed = part * scale * gain_ref[:, lane : lane + w][None]
-            normed = normed.reshape(128, w).astype(BF16)
+            pieces = []
+            for j in range(J):
+                part = R.xc[m, j * TOK : (j + 1) * TOK, lane : lane + w].astype(F32)
+                pieces.append((part * scale * gain_ref[:, j * W + lane : j * W + lane + w]).astype(BF16))
+            normed = jnp.concatenate(pieces, axis=0)
             sz, rz = get("sz", ch), get("rz", ch)
             sz[m] = dot(R.pm[m], normed).astype(BF16)
             mine = pl.ds(pl.multiple_of(z * 16, 16), 16)
@@ -401,23 +414,28 @@
 
     lax.fori_loop(0, MB + 1, turn, 0)
 
-    wait(R.rf, R.rf_r)
-    high, low = combine_matrices(R.rf[pl.ds(s, 1), :], R.rf[pl.ds(s + 4, 1), :])
+    wait(R.rfi, R.rf_r.at[0])
+    wait(R.rfg, R.rf_r.at[1])
+    high, low = combine_matrices(R.rfi[...], R.rfg[...])
     R.cm[MB, 0] = high
     R.cm[MB, 1] = low
     wait(R.xr.at[MB], R.xr_r.at[MB])
     for ch, (lane, w) in enumerate(CHUNKS):
         wait(get("rt", ch).at[MB], get("rtr", ch).at[MB])
-        o_ref[:, lane : lane + w] = combined(MB, ch, lane, w)
+        value = combined(MB, ch, lane, w)
+        for j in range(J):
+            o_ref[:, j * W + lane : j * W + lane + w] = value[j * TOK : (j + 1) * TOK]
 
     @pl.when(s < 3)
     def _():
-        wait(R.rp, R.rp_s)
+        wait(R.rpi, R.rp_s.at[0])
+        wait(R.rpg, R.rp_s.at[1])
 
     @pl.when(s == 3)
     def _():
         for t in range(3):
-            wait(R.rf, R.rf_s.at[t])
+            wait(R.rfi, R.rf_s.at[t, 0])
+            wait(R.rfg, R.rf_s.at[t, 1])
 
     @pl.when(s > 0)
     def _():
@@ -449,28 +467,23 @@
 
 
 def shards(embedded, norm_gain, gate_proj, up_proj, down_proj, expert_ids, route_gates):
-    rows = embedded.reshape(128, W)
-    gain = norm_gain.reshape(J, W)
-    route = jnp.concatenate(
-        [expert_ids.reshape(MB, 128).astype(F32), route_gates.reshape(MB, 128)], axis=0
-    )
     vmem, hbm = pl.BlockSpec(memory_space=pltpu.VMEM), pl.BlockSpec(memory_space=pl.ANY)
     out = pl.pallas_call(
         kernel,
-        out_shape=jax.ShapeDtypeStruct((128, W), BF16),
-        in_specs=[vmem, vmem, vmem, hbm, hbm, hbm],
+        out_shape=jax.ShapeDtypeStruct((TOK, D), BF16),
+        in_specs=[vmem, vmem, vmem, vmem, hbm, hbm, hbm],
         out_specs=vmem,
         scratch_shapes=[shape for _, shape in PLAN],
         compiler_params=pltpu.CompilerParams(
             collective_id=0, has_side_effects=True, vmem_limit_bytes=60 * 1024 * 1024
         ),
         name="expert_sections",
-    )(rows, gain, route, gate_proj[0], up_proj[0], down_proj[0])
-    return out.reshape(1, TOK, D)
+    )(embedded[0], norm_gain, expert_ids[0].swapaxes(1, 2), route_gates[0].swapaxes(1, 2), gate_proj[0], up_proj[0], down_proj[0])
+    return out[None]
 
 
 def solution(mesh):
-    placed = (
+    specs = (
         P("section", "expert", None),
         P("section", None),
         P("section", None, "expert"),
@@ -480,5 +493,5 @@
         P("section", None, "expert", None),
     )
     return jax.shard_map(
-        shards, mesh=mesh, in_specs=placed, out_specs=P("section", "expert", None), check_vma=False
+        shards, mesh=mesh, in_specs=specs, out_specs=P("section", "expert", None), check_vma=False
     )

time: 266 us -> 260 us (0.977)
  local copies, waits for them, and re-layouts: 5.64 us -> 1.64 us
  other arithmetic: 2.78 us -> 0 us
    reshape x4 -> x0, local copies, waits for them, and re-layouts: 4.17 us -> none  [the longest x1 1.73 us: shards(): return out.reshape(1, TOK, D)]
where the time goes in v2:
time: 260 us
  Pallas kernels  258 us (99%)
    pallas_call x1, Pallas kernels, shards(): pl.pallas_call(kernel, out_shape=jax.ShapeDtypeStruct((TOK, D), BF16), in...  258 us

profile of v2, /device:TPU:6, one launch (start us, length us, event | category | flops | bytes accessed | tf_op | source)
XLA Modules:
  0.0 259.7 jit_solution(15540434728550143908)
XLA Ops:
  0.0 258.0 %expert_sections.1 = bf16[16,7168]{1,0:T(8,128)(2,1)} custom-call(bf16[16,7168]{1,0:T(8,128)(2,1)} %bitcast.15, f32[1,7168]{1,0:T(1,128)} %gain_ref.1, s32[4,8,16]{2,1,0:T(8,128)} %bitcast.16, f32[4,8,16]{2,1,0:T(8,128)} %bitcast.17, bf16[7168,256]{1,0:T(8,128)(2,1)} %bitcast.11, bf16[7168,256]{1,0:T(8,128)(2,1)} %bitcast.12, bf16[256,7168]{1,0:T(8,128)(2,1)} %bitcast.13), custom_call_target="tpu_custom_call" | custom-call | tf_op jit(solution)/shard_map/expert_sections/pallas_call | solution.py:471
  258.1 1.6 copy.9

commit v3 on v2

--- a/solution.py
+++ b/solution.py
@@ -404,12 +404,12 @@
             pl.when(cond)(functools.partial(stage, m))
 
         on(back, stage_d, i - 1)
+        on(back, stage_e, i - 1)
         on(front, stage_a, i)
-        on(back, stage_e, i - 1)
+        on(back, stage_f, i - 1)
         on(front, stage_b, i)
-        on(back, stage_f, i - 1)
+        on(back, stage_g, i - 1)
         on(front, stage_c, i)
-        on(back, stage_g, i - 1)
         return carry
 
     lax.fori_loop(0, MB + 1, turn, 0)

time: 260 us -> 233 us (0.90)
  Pallas kernels: 258 us -> 231 us
    pallas_call x1, Pallas kernels: 258 us -> 231 us  [shards(): pl.pallas_call(kernel, out_shape=jax.ShapeDtypeStruct((TOK, D), BF16), in...]
where the time goes in v3:
time: 233 us
  Pallas kernels  231 us (99%)
    pallas_call x1, Pallas kernels, shards(): pl.pallas_call(kernel, out_shape=jax.ShapeDtypeStruct((TOK, D), BF16), in...  231 us

profile of v3, /device:TPU:6, one launch (start us, length us, event | category | flops | bytes accessed | tf_op | source)
XLA Modules:
  0.0 232.8 jit_solution(18390999778161982596)
XLA Ops:
  0.0 231.1 %expert_sections.1 = bf16[16,7168]{1,0:T(8,128)(2,1)} custom-call(bf16[16,7168]{1,0:T(8,128)(2,1)} %bitcast.15, f32[1,7168]{1,0:T(1,128)} %gain_ref.1, s32[4,8,16]{2,1,0:T(8,128)} %bitcast.16, f32[4,8,16]{2,1,0:T(8,128)} %bitcast.17, bf16[7168,256]{1,0:T(8,128)(2,1)} %bitcast.11, bf16[7168,256]{1,0:T(8,128)(2,1)} %bitcast.12, bf16[256,7168]{1,0:T(8,128)(2,1)} %bitcast.13), custom_call_target="tpu_custom_call" | custom-call | tf_op jit(solution)/shard_map/expert_sections/pallas_call | solution.py:471
  231.2 1.6 copy.9
